TPU v7x, 256 devices: a whole 4x4x8 slice. The times are simulated.
256 devices in a mesh: ctx: 32 (over z, x_hi, core), kv: 8 (over y, x_lo).
Axes of the slice: x: 4 (x_hi: 2, x_lo: 2; x = x_hi * 2 + x_lo), y: 4, z: 8, core: 2. Of those that a mesh axis runs over, the one named last changes fastest.
Arguments:
- queries: bfloat16 [6144, 5120], P('ctx', 'kv'), may hold values from -16 to 16
- keys: bfloat16 [6144, 1024], P('ctx', 'kv'), may hold values from -8 to 8
- values: bfloat16 [6144, 1024], P('ctx', 'kv'), may hold values from -6 to 6
- w_out: bfloat16 [5120, 5120], P('kv', 'ctx'), may hold values from -0.078125 to 0.078125
- grad_y: bfloat16 [6144, 5120], P('ctx', 'kv'), may hold values from -6 to 6
- resp_blocks: int32 [4], replicated, may hold values from 1 to 12, 24 in all
Outputs:
- y_out: bfloat16 [6144, 5120], P('ctx', 'kv')
- grad_q: bfloat16 [6144, 5120], P('ctx', 'kv')
- grad_k: bfloat16 [6144, 1024], P('ctx', 'kv')
- grad_v: bfloat16 [6144, 1024], P('ctx', 'kv')
Inputs may be any that keep to these rules, and one draw needn't show every extreme that they name: resp_blocks sums to 24; the longest response has exactly 12 blocks.
All inputs are finite; a program needn't handle non-finite values.
Results may differ from a plain program's by a relative error of at most 0.035.
Values may be sent and summed in bfloat16 or wider, within the bound.
No kernel may reach another device: no remote copies, remote signals or barrier semaphores. Data moves between devices by JAX's collectives and lax.ppermute only.
A program may use at most 64 MiB of HBM per device.

v0:
```python
import math

import jax
import jax.numpy as jnp
from jax import lax
from jax.sharding import PartitionSpec as P

H = 40
KVH = 8
HD = 128
BLK = 128
NRESP = 4


NEG = -1e30


def segment_ids(positions, resp_blocks, prompt_len):
    resp_ends = jnp.cumsum(resp_blocks) * BLK
    offsets = positions - prompt_len
    later = jnp.sum((offsets[:, None] >= resp_ends[None, : NRESP - 1]).astype(jnp.int32), axis=1)
    return jnp.where(positions < prompt_len, 0, 1 + later)


def visible_pairs(query_pos, query_seg, key_pos, key_seg):
    causal = key_pos[None, :] <= query_pos[:, None]
    same = (key_seg[None, :] == 0) | (key_seg[None, :] == query_seg[:, None])
    return causal & same


def local(queries, keys, values, w_out, grad_y, resp_blocks):
    tok_rows = queries.shape[0]
    total_rows = tok_rows * lax.axis_size("ctx")
    prompt_len = total_rows // 2
    group_size = H // KVH
    kv_local = keys.shape[1] // HD
    score_scale = 1.0 / math.sqrt(HD)
    key_block = 4 * BLK
    block_count = total_rows // key_block
    query_pos = lax.axis_index("ctx") * tok_rows + jnp.arange(tok_rows, dtype=jnp.int32)
    query_seg = segment_ids(query_pos, resp_blocks, prompt_len)
    q_four = queries.reshape(tok_rows, kv_local, group_size, HD)
    key_all, value_all = (
        lax.all_gather(keys, "ctx", axis=0, tiled=True),
        lax.all_gather(values, "ctx", axis=0, tiled=True),
    )

    def block_view(block_index):
        first = block_index * key_block
        key_pos = first + jnp.arange(key_block, dtype=jnp.int32)
        key_seg = segment_ids(key_pos, resp_blocks, prompt_len)
        visible = visible_pairs(query_pos, query_seg, key_pos, key_seg)
        key_rows = lax.dynamic_slice_in_dim(key_all, first, key_block, 0).reshape(
            key_block, kv_local, HD
        )
        value_rows = lax.dynamic_slice_in_dim(value_all, first, key_block, 0).reshape(
            key_block, kv_local, HD
        )
        return (visible, key_rows, value_rows)

    def forward_step(state_now, block_index):
        visible, key_rows, value_rows = block_view(block_index)
        run_max, run_sum, run_acc = state_now
        scores = (
            jnp.einsum("tkgd,skd->kgts", q_four, key_rows, preferred_element_type=jnp.float32)
            * score_scale
        )
        masked = jnp.where(visible, scores, NEG)
        new_max = jnp.maximum(run_max, jnp.max(masked, axis=-1))
        weights = jnp.where(visible, jnp.exp(masked - new_max[..., None]), 0.0)
        factor = jnp.exp(run_max - new_max)
        run_sum = run_sum * factor + jnp.sum(weights, axis=-1)
        added = jnp.einsum(
            "kgts,skd->kgtd",
            weights.astype(jnp.bfloat16),
            value_rows,
            preferred_element_type=jnp.float32,
        )
        run_acc = run_acc * factor[..., None] + added
        state_now = (new_max, run_sum, run_acc)
        return (state_now, None)

    start_state = (
        jnp.full((kv_local, group_size, tok_rows), NEG, jnp.float32),
        jnp.zeros((kv_local, group_size, tok_rows), jnp.float32),
        jnp.zeros((kv_local, group_size, tok_rows, HD), jnp.float32),
    )
    (run_max, run_sum, run_acc), unused = lax.scan(
        forward_step, start_state, jnp.arange(block_count, dtype=jnp.int32)
    )
    log_sum = run_max + jnp.log(run_sum)
    attn = (run_acc / run_sum[..., None]).astype(jnp.bfloat16)
    attn_rows = attn.transpose(2, 0, 1, 3).reshape(tok_rows, kv_local * group_size * HD)
    grad_full = lax.all_gather(grad_y, "kv", axis=1, tiled=True)
    weight_all = lax.all_gather(w_out, "ctx", axis=1, tiled=True)
    y_terms = jnp.dot(attn_rows, weight_all, preferred_element_type=jnp.float32)
    grad_attn = lax.dot_general(
        grad_full, weight_all, (((1,), (1,)), ((), ())), preferred_element_type=jnp.float32
    )
    y_out = lax.psum_scatter(y_terms.astype(jnp.bfloat16), "kv", scatter_dimension=1, tiled=True)
    grad_four = grad_attn.astype(jnp.bfloat16).reshape(tok_rows, kv_local, group_size, HD)
    attn_four = attn_rows.reshape(tok_rows, kv_local, group_size, HD)
    delta = jnp.einsum("tkgd,tkgd->kgt", attn_four, grad_four, preferred_element_type=jnp.float32)

    def backward_step(query_grad, block_index):
        visible, key_rows, value_rows = block_view(block_index)
        grad_in = query_grad
        scores = (
            jnp.einsum("tkgd,skd->kgts", q_four, key_rows, preferred_element_type=jnp.float32)
            * score_scale
        )
        masked = jnp.where(visible, scores, NEG)
        probs = jnp.where(visible, jnp.exp(masked - log_sum[..., None]), 0.0)
        value_grad = jnp.einsum(
            "kgts,tkgd->skd",
            probs.astype(jnp.bfloat16),
            grad_four,
            preferred_element_type=jnp.float32,
        )
        prob_grad = jnp.einsum(
            "tkgd,skd->kgts", grad_four, value_rows, preferred_element_type=jnp.float32
        )
        score_grad = (probs * (prob_grad - delta[..., None])).astype(jnp.bfloat16)
        grad_in = (
            grad_in
            + jnp.einsum("kgts,skd->tkgd", score_grad, key_rows, preferred_element_type=jnp.float32)
            * score_scale
        )
        key_grad = (
            jnp.einsum("kgts,tkgd->skd", score_grad, q_four, preferred_element_type=jnp.float32)
            * score_scale
        )
        query_grad, key_grad, value_grad = (grad_in, key_grad, value_grad)
        return (query_grad, (key_grad, value_grad))

    start_grad = jnp.zeros((tok_rows, kv_local, group_size, HD), jnp.float32)
    query_grad, (key_parts, value_parts) = lax.scan(
        backward_step, start_grad, jnp.arange(block_count, dtype=jnp.int32)
    )
    key_terms = key_parts.reshape(total_rows, kv_local * HD)
    value_terms = value_parts.reshape(total_rows, kv_local * HD)
    key_sum, value_sum = (
        lax.psum_scatter(
            key_terms.astype(jnp.bfloat16), "ctx", scatter_dimension=0, tiled=True
        ).astype(jnp.float32),
        lax.psum_scatter(
            value_terms.astype(jnp.bfloat16), "ctx", scatter_dimension=0, tiled=True
        ).astype(jnp.float32),
    )
    grad_q = query_grad.reshape(tok_rows, kv_local * group_size * HD).astype(jnp.bfloat16)
    return (y_out, grad_q, key_sum.astype(jnp.bfloat16), value_sum.astype(jnp.bfloat16))


def solution(mesh):
    placed = (P("ctx", "kv"), P("ctx", "kv"), P("ctx", "kv"), P("kv", "ctx"), P("ctx", "kv"), P())
    return jax.shard_map(
        local,
        mesh=mesh,
        in_specs=placed,
        out_specs=(P("ctx", "kv"), P("ctx", "kv"), P("ctx", "kv"), P("ctx", "kv")),
        check_vma=False,
    )
```

profile of v0, /device:TPU:8, one launch (start us, length us, event | category | flops | bytes accessed | tf_op | source)
XLA Modules:
  0.0 674.9 jit_solution(4073074538010008066)
XLA Ops:
  12.4 80.1 %all-gather.5.cloned.1.call-done = bf16[6144,128]{1,0:T(8,128)(2,1)} async-done(((bf16[192,128]{1,0:T(8,128)(2,1)}), bf16[6144,128]{1,0:T(8,128)(2,1)}) %all-gather.5.cloned.1.call-update) | async-done | bytes 1572880 | tf_op jit(solution)/shard_map/all_gather | solution.py:44
  92.5 78.0 %all-gather.7.cloned.1.call-done = bf16[6144,128]{1,0:T(8,128)(2,1)} async-done(((bf16[192,128]{1,0:T(8,128)(2,1)}), bf16[6144,128]{1,0:T(8,128)(2,1)}) %all-gather.7.cloned.1.call-update) | async-done | bytes 1572880 | tf_op jit(solution)/shard_map/all_gather | solution.py:45
  170.5 67.2 %while.34 = (s32[]{:T(128)}, f32[1,5,192]{2,1,0:T(8,128)S(1)}, f32[1,5,192]{2,1,0:T(8,128)S(1)}, f32[1,5,192,128]{3,2,1,0:T(8,128)S(1)}, s32[12]{0:T(128)S(1)}, ...) while((s32[]{:T(128)}, f32[1,5,192]{2,1,0:T(8,128)S(1)}, ...), condition=%wide.region_6.7_spmd.clone, body=%wide.region_2.6_spmd.clone.sunk | while | flops 258823488 | bytes 7863859 | solution.py:88
  172.0 1.5 fusion.87
  174.3 1.7 fusion.90
  177.6 1.5 fusion.87
  179.9 1.7 fusion.90
  183.2 1.5 fusion.87
  185.5 1.7 fusion.90
  188.8 1.5 fusion.87
  191.1 1.7 fusion.90
  194.4 1.5 fusion.87
  196.7 1.7 fusion.90
  200.0 1.5 fusion.87
  202.3 1.7 fusion.90
  205.7 1.5 fusion.87
  207.9 1.7 fusion.90
  211.3 1.5 fusion.87
  213.5 1.7 fusion.90
  216.9 1.5 fusion.87
  219.1 1.7 fusion.90
  222.5 1.5 fusion.87
  224.7 1.7 fusion.90
  228.1 1.5 fusion.87
  230.3 1.7 fusion.90
  233.7 1.5 fusion.87
  235.9 1.8 fusion.90
  238.4 79.6 %all-gather.9.cloned.1.call-done = bf16[640,5120]{0,1:T(8,128)(2,1)} async-done(((bf16[640,160]{0,1:T(8,128)(2,1)}), bf16[640,5120]{0,1:T(8,128)(2,1)}) %all-gather.9.cloned.1.call-update) | async-done | bytes 6553616 | tf_op jit(solution)/shard_map/all_gather | solution.py:95
  318.0 5.2 convolution_convert_fusion.1
  323.5 6.7 convolution_convert_fusion
  330.2 4.3 copy.46
  334.6 99.3 %while.35 = (s32[]{:T(128)}, f32[192,1,5,128]{3,0,2,1:T(8,128)S(1)}, bf16[12,512,1,128]{3,1,2,0:T(8,128)(2,1)}, bf16[12,512,1,128]{3,1,2,0:T(8,128)(2,1)}, s32[1...) while((s32[]{:T(128)}, ...), condition=%wide.region_10.11_spmd.clone, body=%wide.region_8.10_spmd.clone.sunk | while | flops 633913024 | bytes 11955285 | solution.py:137
  336.2 1.6 fusion.101
  344.5 1.6 fusion.101
  348.6 1.4 fusion.103
  352.8 1.6 fusion.101
  361.0 1.6 fusion.101
  369.3 1.6 fusion.101
  377.6 1.6 fusion.101
  385.9 1.6 fusion.101
  394.1 1.6 fusion.101
  402.4 1.6 fusion.101
  410.7 1.6 fusion.101
  419.0 1.6 fusion.101
  427.2 1.6 fusion.101
  435.8 1.8 copy.47
  437.6 110.5 %reduce-scatter.8.cloned.1.call-done = bf16[192,128]{1,0:T(8,128)(2,1)} async-done(((bf16[6144,128]{1,0:T(8,128)(2,1)}), bf16[192,128]{1,0:T(8,128)(2,1)}) %reduce-scatter.8.cloned.1.call-update) | async-done | bytes 49168 | tf_op jit(solution)/shard_map/reduce_scatter | solution.py:146
  548.1 120.0 %reduce-scatter.6.cloned.1.call-done = bf16[192,128]{1,0:T(8,128)(2,1)} async-done(((bf16[6144,128]{1,0:T(8,128)(2,1)}), bf16[192,128]{1,0:T(8,128)(2,1)}) %reduce-scatter.6.cloned.1.call-update) | async-done | bytes 49168 | tf_op jit(solution)/shard_map/reduce_scatter | solution.py:143
  (329 shorter events, 97.9 us)
Async XLA Ops:
  7.2 85.3 %all-gather.5.cloned.1.call-start = ((), (), s32[]{:S(2)}) async-start(), calls=%async_computation.3 | async-start | bytes 1622016 | tf_op jit(solution)/shard_map/all_gather | solution.py:44
  7.9 162.6 %all-gather.7.cloned.1.call-start = ((), (), s32[]{:S(2)}) async-start(), calls=%async_computation.4 | async-start | bytes 1622016 | tf_op jit(solution)/shard_map/all_gather | solution.py:45
  8.6 229.7 %all-gather.11.cloned.1.call-start = ((), (), s32[]{:S(2)}) async-start(), calls=%async_computation.6 | async-start | bytes 2211840 | tf_op jit(solution)/shard_map/all_gather | solution.py:94
  9.4 308.6 %all-gather.9.cloned.1.call-start = ((), (), s32[]{:S(2)}) async-start(), calls=%async_computation.5 | async-start | bytes 6758400 | tf_op jit(solution)/shard_map/all_gather | solution.py:95
  10.0 425.9 %reduce-scatter.10.cloned.1.call-start = ((), (), s32[]{:S(2)}) async-start(), calls=%async_computation.9 | async-start | bytes 2949120
  334.5 213.6 %reduce-scatter.8.cloned.1.call-start = ((), (), s32[]{:S(2)}) async-start(), calls=%async_computation.8 | async-start | bytes 1622016 | tf_op jit(solution)/shard_map/reduce_scatter | solution.py:146
  434.0 234.1 %reduce-scatter.6.cloned.1.call-start = ((), (), s32[]{:S(2)}) async-start(), calls=%async_computation.7 | async-start | bytes 1622016 | tf_op jit(solution)/shard_map/reduce_scatter | solution.py:143
Sparse Core Ops, SparseCore 0:
  10.8 81.6 all-gather.4
  95.3 75.1 all-gather.6
  172.3 46.8 all-gather.10
  221.8 96.1 all-gather.8
  334.6 59.7 reduce-scatter.9
  434.1 113.9 reduce-scatter.7
  552.8 115.2 reduce-scatter.5
where the time goes:
time: 676 us; the launch traced here: 675 us
  waiting for transfers between devices  471 us (70%)
  matrix products  131 us (19%)
  local copies, waits for them, and re-layouts  23.4 us (3%)
  loops' own time  17.5 us (3%)
  other arithmetic  17.3 us (3%)
  between operations  14.3 us (2%)
    reduce_scatter x1, waiting for transfers between devices, local(): lax.psum_scatter(key_terms.astype(jnp.bfloat16), 'ctx', scatter_dimension...  120 us
    reduce_scatter x1, waiting for transfers between devices, local(): lax.psum_scatter(value_terms.astype(jnp.bfloat16), 'ctx', scatter_dimensi...  110 us
    all_gather x1, waiting for transfers between devices, local(): lax.all_gather(keys, 'ctx', axis=0, tiled=True)  80.1 us
    all_gather x1, waiting for transfers between devices, local(): weight_all = lax.all_gather(w_out, 'ctx', axis=1, tiled=True)  79.6 us
    all_gather x1, waiting for transfers between devices, local(): lax.all_gather(values, 'ctx', axis=0, tiled=True)  78 us
    dot_general x12, matrix products, forward_step(): jnp.einsum('kgts,skd->kgtd', weights.astype(jnp.bfloat16), value_rows, pr...  21 us
    dot_general x12, matrix products, backward_step(): jnp.einsum('tkgd,skd->kgts', q_four, key_rows, preferred_element_type=jnp...  19.2 us
    dot_general x12, matrix products, forward_step(): jnp.einsum('tkgd,skd->kgts', q_four, key_rows, preferred_element_type=jnp...  17.7 us
  transfers between devices with their start and end apart: 7, of which 5 were waited for; matrix products, arithmetic and copies ran while one was open for 23% of the time, Pallas kernels for 0%

commit v1 on v0

v1 whole, which is shorter than its diff:
```python
import math

import jax
import jax.numpy as jnp
from jax import lax
from jax.experimental import pallas as pl
from jax.experimental.pallas import tpu as pltpu
from jax.sharding import Mesh
from jax.sharding import PartitionSpec as P

GROUP = 5
HD = 128
BLK = 128
NRESP = 4
NZ = 8
TOK = 192
ROWS = 1024
TILE = 256
HALF = 2 * TOK
CHUNK = 4 * TOK
PROMPT = 4 * CHUNK
NEG = -1e30
SCALE = 1.0 / math.sqrt(HD)
SCALE2 = SCALE * math.log2(math.e)
CTX = ("z", "xh", "c")
KV = ("y", "xl")
F32 = jnp.float32
BF16 = jnp.bfloat16


def shift(x, axis, by, size):
    return lax.ppermute(x, axis, [(i, (i + by) % size) for i in range(size)])


def dot(a, b):
    return jnp.dot(a, b, preferred_element_type=F32)


def ring_gather(own):
    rows = own.shape[0] // 2
    up, down = own, own
    blocks = {0: own}
    for step in range(1, NZ // 2):
        up, down = shift(up, "z", 1, NZ), shift(down, "z", -1, NZ)
        blocks[NZ - step], blocks[step] = up, down
    far_up = shift(up[:rows], "z", 1, NZ)
    far_down = shift(down[rows:], "z", -1, NZ)
    blocks[NZ // 2] = jnp.concatenate([far_up, far_down], 0)
    return [blocks[k] for k in range(NZ)]


def add(a, b):
    return (a.astype(F32) + b.astype(F32)).astype(BF16)


def ring_reduce(parts):
    rows = parts[0].shape[0] // 2
    far = NZ // 2
    up = shift(parts[far][:rows], "z", 1, NZ)
    down = shift(parts[far][rows:], "z", -1, NZ)
    up = jnp.concatenate([add(parts[far - 1][:rows], up), parts[far - 1][rows:]], 0)
    down = jnp.concatenate([parts[far + 1][:rows], add(parts[far + 1][rows:], down)], 0)
    up, down = shift(up, "z", 1, NZ), shift(down, "z", -1, NZ)
    for step in range(far - 2, 0, -1):
        up, down = add(parts[step], up), add(parts[NZ - step], down)
        up, down = shift(up, "z", 1, NZ), shift(down, "z", -1, NZ)
    return parts[0].astype(F32) + (up.astype(F32) + down.astype(F32))


def head_rows(x_ref, rows_ref):
    for h in range(GROUP):
        rows_ref[h * TOK : (h + 1) * TOK, :] = x_ref[:, h * HD : (h + 1) * HD]
    rows_ref[GROUP * TOK :, :] = jnp.zeros((ROWS - GROUP * TOK, HD), rows_ref.dtype)


def flip(x):
    return x.astype(F32).T


def visible_tile(pos, qinfo_ref, tile, chunk):
    cols = slice(tile * TILE, (tile + 1) * TILE)
    query_pos = qinfo_ref[0:1, cols]
    first = jnp.where(chunk < PROMPT // CHUNK, 0, qinfo_ref[1:2, cols])
    return (pos <= query_pos) & (pos >= first)


def forward_kernel(
    flags_ref, chunk_ref, q_ref, mine_ref, other_ref, posr_ref, qinfo_ref,
    attn_ref, attn_t_ref, lse_ref, rows_ref, q_t_ref, top_ref, sum_ref, acc_ref,
):
    head_rows(q_ref, rows_ref)
    q_t_ref[...] = flip(rows_ref[...]).astype(BF16)
    top_ref[...] = jnp.full_like(top_ref, NEG)
    sum_ref[...] = jnp.zeros_like(sum_ref)
    acc_ref[...] = jnp.zeros_like(acc_ref)

    def step(k, masked):
        chunk = chunk_ref[k]
        at = pl.ds(pl.multiple_of(k * HALF, HALF), HALF)
        both = jnp.concatenate([mine_ref[at, :], other_ref[at, :]], 0)
        keys, values = both[:, :HD], both[:, HD:]
        values_t = flip(values).astype(BF16)
        pos = posr_ref[:, 0:1] + chunk * CHUNK
        for tile in range(ROWS // TILE):
            cols = slice(tile * TILE, (tile + 1) * TILE)
            scores = dot(keys, q_t_ref[:, cols]) * SCALE2
            if masked:
                scores = jnp.where(visible_tile(pos, qinfo_ref, tile, chunk), scores, NEG)
            old = top_ref[0:1, cols]
            top = jnp.maximum(old, jnp.max(scores, axis=0, keepdims=True))
            weights = jnp.exp2(scores - top)
            factor = jnp.exp2(old - top)
            top_ref[0:1, cols] = top
            sum_ref[0:1, cols] = sum_ref[0:1, cols] * factor + jnp.sum(weights, axis=0, keepdims=True)
            acc_ref[:, cols] = acc_ref[:, cols] * factor + dot(values_t, weights.astype(BF16))

    def body(k, carry):
        @pl.when(flags_ref[k] == 1)
        def _():
            step(k, False)

        @pl.when(flags_ref[k] == 2)
        def _():
            step(k, True)

        return carry

    lax.fori_loop(0, NZ, body, 0)
    lse_ref[...] = jnp.broadcast_to(top_ref[0:1, :] + jnp.log2(sum_ref[0:1, :]), lse_ref.shape)
    attn_t = acc_ref[...] / sum_ref[0:1, :]
    attn_t_ref[...] = attn_t.astype(BF16)
    attn = attn_t.T.astype(BF16)
    for h in range(GROUP):
        attn_ref[:, h * HD : (h + 1) * HD] = attn[h * TOK : (h + 1) * TOK, :]


def backward_kernel(
    flags_ref, chunk_ref, q_ref, g_ref, mine_ref, other_ref, posr_ref, qinfo_ref, attn_t_ref, lse_ref,
    dq_ref, dmine_ref, dother_ref, rows_ref, q_t_ref, g_rows_ref, g_t_ref, delta_ref, dq_t_ref, dk_ref, dv_ref,
):
    head_rows(q_ref, rows_ref)
    q_t_ref[...] = flip(rows_ref[...]).astype(BF16)
    head_rows(g_ref, g_rows_ref)
    g_t = flip(g_rows_ref[...])
    g_t_ref[...] = g_t.astype(BF16)
    delta_ref[0:1, :] = jnp.sum(g_t * attn_t_ref[...].astype(F32), axis=0, keepdims=True)
    dq_t_ref[...] = jnp.zeros_like(dq_t_ref)

    def step(k, masked):
        chunk = chunk_ref[k]
        at = pl.ds(pl.multiple_of(k * HALF, HALF), HALF)
        both = jnp.concatenate([mine_ref[at, :], other_ref[at, :]], 0)
        keys, values = both[:, :HD], both[:, HD:]
        keys_t = flip(keys).astype(BF16)
        pos = posr_ref[:, 0:1] + chunk * CHUNK
        for tile in range(ROWS // TILE):
            cols = slice(tile * TILE, (tile + 1) * TILE)
            scores = dot(keys, q_t_ref[:, cols]) * SCALE2
            if masked:
                scores = jnp.where(visible_tile(pos, qinfo_ref, tile, chunk), scores, NEG)
            probs = jnp.exp2(scores - lse_ref[0:1, cols])
            dv = dot(probs.astype(BF16), g_rows_ref[cols, :])
            grads = probs * (dot(values, g_t_ref[:, cols]) - delta_ref[0:1, cols])
            grads = grads.astype(BF16)
            dk = dot(grads, rows_ref[cols, :])
            dv_ref[...] = dv if tile == 0 else dv_ref[...] + dv
            dk_ref[...] = dk if tile == 0 else dk_ref[...] + dk
            dq_t_ref[:, cols] += dot(keys_t, grads)
        dk, dv = (dk_ref[...] * SCALE).astype(BF16), dv_ref[...].astype(BF16)
        dmine_ref[at, :HD] = dk[:HALF]
        dmine_ref[at, HD:] = dv[:HALF]
        dother_ref[at, :HD] = dk[HALF:]
        dother_ref[at, HD:] = dv[HALF:]

    def body(k, carry):
        @pl.when(flags_ref[k] == 0)
        def _():
            at = pl.ds(pl.multiple_of(k * HALF, HALF), HALF)
            dmine_ref[at, :] = jnp.zeros((HALF, 2 * HD), BF16)
            dother_ref[at, :] = jnp.zeros((HALF, 2 * HD), BF16)

        @pl.when(flags_ref[k] == 1)
        def _():
            step(k, False)

        @pl.when(flags_ref[k] == 2)
        def _():
            step(k, True)

        return carry

    lax.fori_loop(0, NZ, body, 0)
    dq = (dq_t_ref[...].T * SCALE).astype(BF16)
    for h in range(GROUP):
        dq_ref[:, h * HD : (h + 1) * HD] = dq[h * TOK : (h + 1) * TOK, :]


SMEM = pl.BlockSpec(memory_space=pltpu.SMEM)
VMEM = pl.BlockSpec(memory_space=pltpu.VMEM)
PARAMS = pltpu.CompilerParams(vmem_limit_bytes=48 << 20)


def forward(flags, chunks, q, mine, other, posr, qinfo):
    return pl.pallas_call(
        forward_kernel,
        out_shape=(
            jax.ShapeDtypeStruct((TOK, GROUP * HD), BF16),
            jax.ShapeDtypeStruct((HD, ROWS), BF16),
            jax.ShapeDtypeStruct((8, ROWS), F32),
        ),
        in_specs=[SMEM, SMEM] + [VMEM] * 5,
        out_specs=(VMEM,) * 3,
        scratch_shapes=[
            pltpu.VMEM((ROWS, HD), BF16),
            pltpu.VMEM((HD, ROWS), BF16),
            pltpu.VMEM((8, ROWS), F32),
            pltpu.VMEM((8, ROWS), F32),
            pltpu.VMEM((HD, ROWS), F32),
        ],
        compiler_params=PARAMS,
        cost_estimate=pl.CostEstimate(flops=4 * 960 * 4608 * 128, bytes_accessed=4 << 20, transcendentals=960 * 4608),
        name="forward",
    )(flags, chunks, q, mine, other, posr, qinfo)


def backward(flags, chunks, q, g, mine, other, posr, qinfo, attn_t, lse):
    return pl.pallas_call(
        backward_kernel,
        out_shape=(
            jax.ShapeDtypeStruct((TOK, GROUP * HD), BF16),
            jax.ShapeDtypeStruct((NZ * HALF, 2 * HD), BF16),
            jax.ShapeDtypeStruct((NZ * HALF, 2 * HD), BF16),
        ),
        in_specs=[SMEM, SMEM] + [VMEM] * 8,
        out_specs=(VMEM,) * 3,
        scratch_shapes=[
            pltpu.VMEM((ROWS, HD), BF16),
            pltpu.VMEM((HD, ROWS), BF16),
            pltpu.VMEM((ROWS, HD), BF16),
            pltpu.VMEM((HD, ROWS), BF16),
            pltpu.VMEM((8, ROWS), F32),
            pltpu.VMEM((HD, ROWS), F32),
            pltpu.VMEM((CHUNK, HD), F32),
            pltpu.VMEM((CHUNK, HD), F32),
        ],
        compiler_params=PARAMS,
        cost_estimate=pl.CostEstimate(flops=10 * 960 * 4608 * 128, bytes_accessed=8 << 20, transcendentals=960 * 4608),
        name="backward",
    )(flags, chunks, q, g, mine, other, posr, qinfo, attn_t, lse)


def tables(resp_blocks):
    z, xh, c = lax.axis_index("z"), lax.axis_index("xh"), lax.axis_index("c")
    row = jnp.arange(CHUNK, dtype=jnp.int32)
    core = jnp.where(row < HALF, c, 1 - c)
    posr = core * TOK + (row % HALF) // TOK * HALF + row % TOK
    posr = jnp.broadcast_to(posr[:, None], (CHUNK, 128))
    first = z * CHUNK + xh * HALF + c * TOK
    query_pos = first + jnp.arange(ROWS, dtype=jnp.int32) % TOK
    end, start = jnp.int32(PROMPT), jnp.full((ROWS,), PROMPT, jnp.int32)
    for r in range(NRESP - 1):
        end = end + resp_blocks[r] * BLK
        start = jnp.where(query_pos >= end, end, start)
    qinfo = jnp.concatenate(
        [query_pos[None], start[None], jnp.zeros((6, ROWS), jnp.int32)], 0
    )
    chunks = (z + jnp.arange(NZ, dtype=jnp.int32)) % NZ
    earlier = (chunks < PROMPT // CHUNK) | ((chunks + 1) * CHUNK > jnp.min(start))
    kind = jnp.where(chunks < PROMPT // CHUNK, 1, 2)
    flags = jnp.where(chunks == z, 2, jnp.where((chunks < z) & earlier, kind, 0))
    return flags, chunks, posr, qinfo


def local(queries, keys, values, w_out, grad_y, resp_blocks):
    xh = lax.axis_index("xh")
    flags, chunks, posr, qinfo = tables(resp_blocks)
    weight = lax.all_gather(w_out.T, CTX, axis=0, tiled=True)
    grad_full = lax.all_gather(grad_y, KV, axis=1, tiled=True)

    own = jnp.concatenate([keys, values], 1)
    partner = shift(own, "xh", 1, 2)
    own = jnp.where(xh == 0, jnp.concatenate([own, partner], 0), jnp.concatenate([partner, own], 0))
    mine = jnp.concatenate(ring_gather(own), 0)
    other = shift(mine, "c", 1, 2)

    attn, attn_t, lse = forward(flags, chunks, queries, mine, other, posr, qinfo)
    grad_attn = dot(grad_full, weight).astype(BF16)
    y_terms = lax.dot_general(attn, weight, (((1,), (1,)), ((), ())), preferred_element_type=F32).astype(BF16)
    y_out = lax.psum_scatter(y_terms, KV, scatter_dimension=1, tiled=True)
    grad_q, dmine, dother = backward(
        flags, chunks, queries, grad_attn, mine, other, posr, qinfo, attn_t, lse
    )
    terms = add(dmine, shift(dother, "c", 1, 2))
    total = ring_reduce([terms[k * HALF : (k + 1) * HALF] for k in range(NZ)])
    low, high = total[:TOK], total[TOK:]
    send = jnp.where(xh == 0, high, low).astype(BF16)
    total = jnp.where(xh == 0, low, high) + shift(send, "xh", 1, 2).astype(F32)
    total = total.astype(BF16)
    return y_out, grad_q, total[:, :HD], total[:, HD:]


def solution(mesh):
    fine = Mesh(mesh.devices.reshape(NZ, 2, 2, 4, 2), CTX + KV)
    both = P(CTX, KV)
    return jax.shard_map(
        local,
        mesh=fine,
        in_specs=(both, both, both, P(KV, CTX), both, P()),
        out_specs=(both,) * 4,
        check_vma=False,
    )
```

time: 676 us -> 266 us (0.39)
  waiting for transfers between devices: 471 us -> 173 us
  matrix products: 131 us -> 8.99 us
  starting transfers between devices: 0.27 us -> 41.7 us
  loops' own time: 17.5 us -> 0 us
  local copies, waits for them, and re-layouts: 23.4 us -> 9.41 us
  other arithmetic: 17.3 us -> 3.71 us
  Pallas kernels: 0 us -> 9.96 us
    reduce_scatter x2 -> x0, waiting for transfers between devices: 230 us -> none  [the longest x1 120 us: local(): lax.psum_scatter(key_terms.astype(jnp.bfloat16), 'ctx', scatter_dimension...]
    all_gather x4 -> x2, waiting for transfers between devices: 238 us -> 107 us  [the longest x1 98.9 us: local(): weight = lax.all_gather(w_out.T, CTX, axis=0, tiled=True)]
    dot_general x86 -> x2, matrix products: 131 us -> 8.99 us  [the longest x1 5.3 us: dot(): return jnp.dot(a, b, preferred_element_type=F32)]
    ppermute x0 -> x20, waiting for transfers between devices: none -> 47.2 us  [shift(): return lax.ppermute(x, axis, [(i, (i + by) % size) for i in range(size)])]
    ppermute x0 -> x20, starting transfers between devices: none -> 41.5 us  [shift(): return lax.ppermute(x, axis, [(i, (i + by) % size) for i in range(size)])]
    another operation x2 -> x0, loops' own time: 17.5 us -> none  [the longest x1 8.84 us: local(): lax.scan(forward_step, start_state, jnp.arange(block_count, dtype=jnp.int...]
    unnamed x8 -> x4, waiting for transfers between devices: 3.31 us -> 18.9 us
    dynamic_slice x24 -> x0, local copies, waits for them, and re-layouts: 14.1 us -> none  [local(): lax.scan(forward_step, start_state, jnp.arange(block_count, dtype=jnp.int...]
  transfers between devices with their start and end apart: 7 -> 23, of which waited for: 5 -> 14; matrix products, arithmetic and copies ran while one was open for 23% -> 6% of each run, Pallas kernels for 0% -> 2%
where the time goes in v1:
time: 266 us; the launch traced here: 263 us
  waiting for transfers between devices  173 us (65%)
  starting transfers between devices  41.7 us (16%)
  between operations  16 us (6%)
  Pallas kernels  9.96 us (4%)
  local copies, waits for them, and re-layouts  9.41 us (4%)
  matrix products  8.99 us (3%)
  other arithmetic  3.71 us (1%)
    all_gather x1, waiting for transfers between devices, local(): weight = lax.all_gather(w_out.T, CTX, axis=0, tiled=True)  98.9 us
    ppermute x20, waiting for transfers between devices, shift(): return lax.ppermute(x, axis, [(i, (i + by) % size) for i in range(size)])  47.2 us
    ppermute x20, starting transfers between devices, shift(): return lax.ppermute(x, axis, [(i, (i + by) % size) for i in range(size)])  41.5 us
    unnamed x4, waiting for transfers between devices  18.9 us
    all_gather x1, waiting for transfers between devices, local(): grad_full = lax.all_gather(grad_y, KV, axis=1, tiled=True)  8.28 us
    unnamed x22, local copies, waits for them, and re-layouts  7.01 us
    pallas_call x1, Pallas kernels, backward(): pl.pallas_call(backward_kernel, out_shape=(jax.ShapeDtypeStruct((TOK, GRO...  5.75 us
  transfers between devices with their start and end apart: 23, of which 14 were waited for; matrix products, arithmetic and copies ran while one was open for 6% of the time, Pallas kernels for 2%

profile of v1, /device:TPU:8, one launch (start us, length us, event | category | flops | bytes accessed | tf_op | source)
XLA Modules:
  0.0 263.0 jit_solution(3350919713911032137)
XLA Ops:
  7.2 0.7 all-gather.5.cloned.1.call-update
  7.9 0.7 all-gather.3.cloned.1.call-update
  8.7 0.8 constant_dynamic-update-slice_fusion.1
  9.5 0.8 constant_dynamic-update-slice_fusion
  10.3 3.1 %collective-permute-start = (bf16[192,256]{1,0:T(8,128)(2,1)S(1)}, bf16[192,256]{1,0:T(8,128)(2,1)S(1)}, u32[]{:S(2)}, u32[]{:S(2)}) collective-permute-start(bf16[192,256]{1,0:T(8,128)(2,1)S(1)} %constant_dynamic-update-slice_fusion), channel_id=1, source_target_pairs={{0,16},{16,0},{1,17},{17,1},{2,18},{18,2},{3,19},{19,3},{4,20},{20... | collective-permute-start | bytes 294920 | tf_op jit(solution)/shard_map/ppermute | solution.py:32
  13.4 3.1 %collective-permute-done = bf16[192,256]{1,0:T(8,128)(2,1)S(1)} collective-permute-done((bf16[192,256]{1,0:T(8,128)(2,1)S(1)}, bf16[192,256]{1,0:T(8,128)(2,1)S(1)}, u32[]{:S(2)}, u32[]{:S(2)}) %collective-permute-start) | collective-permute-done | bytes 98336 | tf_op jit(solution)/shard_map/ppermute | solution.py:32
  16.6 2.0 collective-permute-start.4
  18.6 4.0 %collective-permute-start.1 = (bf16[384,256]{1,0:T(8,128)(2,1)S(1)}, bf16[384,256]{1,0:T(8,128)(2,1)S(1)}, u32[]{:S(2)}, u32[]{:S(2)}) collective-permute-start(bf16[384,256]{1,0:T(8,128)(2,1)S(1)} %get-tuple-element.17), channel_id=1, source_target_pairs={{0,224},{32,0},{64,32},{96,64},{128,96},{160,128},{192,160},{224,1... | collective-permute-start | bytes 589832 | tf_op jit(solution)/shard_map/ppermute | solution.py:32
  22.6 3.7 %collective-permute-done.4 = bf16[384,256]{1,0:T(8,128)(2,1)S(1)} collective-permute-done((bf16[384,256]{1,0:T(8,128)(2,1)S(1)}, bf16[384,256]{1,0:T(8,128)(2,1)S(1)}, u32[]{:S(2)}, u32[]{:S(2)}) %collective-permute-start.4) | collective-permute-done | bytes 196640 | tf_op jit(solution)/shard_map/ppermute | solution.py:32
  26.3 3.2 %collective-permute-start.2 = (bf16[384,256]{1,0:T(8,128)(2,1)S(1)}, bf16[384,256]{1,0:T(8,128)(2,1)S(1)}, u32[]{:S(2)}, u32[]{:S(2)}) collective-permute-start(bf16[384,256]{1,0:T(8,128)(2,1)S(1)} %collective-permute-done.1), channel_id=1, source_target_pairs={{0,224},{32,0},{64,32},{96,64},{128,96},{160,128},{192,160},{224,1... | collective-permute-start | bytes 589832 | tf_op jit(solution)/shard_map/ppermute | solution.py:32
  29.5 3.6 %collective-permute-done.5 = bf16[384,256]{1,0:T(8,128)(2,1)S(1)} collective-permute-done((bf16[384,256]{1,0:T(8,128)(2,1)S(1)}, bf16[384,256]{1,0:T(8,128)(2,1)S(1)}, u32[]{:S(2)}, u32[]{:S(2)}) %collective-permute-start.5) | collective-permute-done | bytes 196640 | tf_op jit(solution)/shard_map/ppermute | solution.py:32
  33.2 3.2 %collective-permute-start.3 = (bf16[384,256]{1,0:T(8,128)(2,1)S(1)}, bf16[384,256]{1,0:T(8,128)(2,1)S(1)}, u32[]{:S(2)}, u32[]{:S(2)}) collective-permute-start(bf16[384,256]{1,0:T(8,128)(2,1)S(1)} %collective-permute-done.2), channel_id=1, source_target_pairs={{0,224},{32,0},{64,32},{96,64},{128,96},{160,128},{192,160},{224,1... | collective-permute-start | bytes 589832 | tf_op jit(solution)/shard_map/ppermute | solution.py:32
  36.4 3.6 %collective-permute-done.6 = bf16[384,256]{1,0:T(8,128)(2,1)S(1)} collective-permute-done((bf16[384,256]{1,0:T(8,128)(2,1)S(1)}, bf16[384,256]{1,0:T(8,128)(2,1)S(1)}, u32[]{:S(2)}, u32[]{:S(2)}) %collective-permute-start.6) | collective-permute-done | bytes 196640 | tf_op jit(solution)/shard_map/ppermute | solution.py:32
  40.0 0.1 collective-permute-start.7
  40.2 3.3 %collective-permute-start.8 = (bf16[192,256]{1,0:T(8,128)(2,1)S(1)}, bf16[192,256]{1,0:T(8,128)(2,1)S(1)}, u32[]{:S(2)}, u32[]{:S(2)}) collective-permute-start(bf16[192,256]{1,0:T(8,128)(2,1)S(1)} %slice.90), channel_id=1, source_target_pairs={{0,224},{32,0},{64,32},{96,64},{128,96},{160,128},{192,160},{224,1... | collective-permute-start | bytes 294920 | tf_op jit(solution)/shard_map/ppermute | solution.py:32
  43.5 2.5 collective-permute-done.7
  46.1 0.3 collective-permute-start.9
  46.4 0.6 fusion.21
  49.1 0.6 select_reduce_fusion
  49.7 0.7 compare_select_fusion.5
  50.5 0.2 broadcast_in_dim.42.posr_ref
  50.7 4.2 %forward.1 = (bf16[192,640]{1,0:T(8,128)(2,1)S(1)}, bf16[128,1024]{1,0:T(8,128)(2,1)S(1)}, f32[8,1024]{1,0:T(8,128)S(1)}) custom-call(s32[8]{0:T(128)S(1)} %get-tuple-element.31.flags_ref, s32[8]{0:T(128)S(1)} %get-tuple-element.32.chunk_ref, bf16[192,640]{1,0:T(8,128)(2,1)S(1)} %copy-done.2, ...), custom_call_target="tpu_custom_call" | custom-call | flops 2264924160 | bytes 4194304 | tf_op jit(solution)/shard_map/forward/pallas_call | solution.py:204
  54.9 8.3 %all-gather.5.cloned.1.call-done = bf16[192,5120]{1,0:T(8,128)(2,1)} async-done(((bf16[192,640]{1,0:T(8,128)(2,1)}), bf16[192,5120]{1,0:T(8,128)(2,1)}) %all-gather.5.cloned.1.call-update) | async-done | bytes 1966096 | tf_op jit(solution)/shard_map/all_gather | solution.py:278
  63.2 98.9 %all-gather.3.cloned.1.call-done = bf16[5120,640]{1,0:T(8,128)(2,1)} async-done(((bf16[160,640]{1,0:T(8,128)(2,1)}), bf16[5120,640]{1,0:T(8,128)(2,1)}) %all-gather.3.cloned.1.call-update) | async-done | bytes 6553616 | tf_op jit(solution)/shard_map/all_gather | solution.py:277
  162.1 5.3 %convolution_convert_fusion.1.g_ref = bf16[192,640]{1,0:T(8,128)(2,1)S(1)} fusion(bf16[192,5120]{1,0:T(8,128)(2,1)} %all-gather.5.cloned.1.call-done, bf16[5120,640]{1,0:T(8,128)(2,1)} %all-gather.3.cloned.1.call-done), kind=kOutput, calls=%fused_computation.2 | convolution fusion | flops 1258414080 | bytes 8765440 | tf_op jit(solution)/shard_map/dot_general | solution.py:36
  167.5 5.7 %backward.1 = (bf16[192,640]{1,0:T(8,128)(2,1)}, bf16[3072,256]{1,0:T(8,128)(2,1)S(1)}, bf16[3072,256]{1,0:T(8,128)(2,1)}) custom-call(s32[8]{0:T(128)S(1)} %get-tuple-element.31.flags_ref, s32[8]{0:T(128)S(1)} %get-tuple-element.32.chunk_ref, bf16[192,640]{1,0:T(8,128)(2,1)S(1)} %copy-done.2, bf16[192,640]{1,0:T(8,128)(2,1)S(1)} %convolution_convert_fusion.1.g_ref, ...), custom_call_target="tpu_custom_call" | custom-call | flops 5662310400 | bytes 8388608 | tf_op jit(solution)/shard_map/backward/pallas_call | solution.py:227
  173.2 0.3 collective-permute-start.10
  173.5 3.7 %convolution_convert_fusion = bf16[192,5120]{1,0:T(8,128)(2,1)} fusion(bf16[192,640]{1,0:T(8,128)(2,1)S(1)} %get-tuple-element.10, bf16[5120,640]{1,0:T(8,128)(2,1)S(1)} %bitcast.14), kind=kOutput, calls=%fused_computation | convolution fusion | flops 1259274240 | bytes 8765440 | tf_op jit(solution)/shard_map/dot_general | solution.py:288
  177.2 4.3 %copy.10 = bf16[192,5120]{0,1:T(8,128)(2,1)} copy(bf16[192,5120]{1,0:T(8,128)(2,1)} %convolution_convert_fusion) | data formatting | bytes 3932160
  181.5 1.8 add_convert_fusion
  183.3 3.4 %collective-permute-start.11 = (bf16[192,256]{1,0:T(8,128)(2,1)S(1)}, bf16[192,256]{1,0:T(8,128)(2,1)S(1)}, u32[]{:S(2)}, u32[]{:S(2)}) collective-permute-start(bf16[192,256]{1,0:T(8,128)(2,1)S(1)} %get-tuple-element.22), channel_id=1, source_target_pairs={{0,32},{32,64},{64,96},{96,128},{128,160},{160,192},{192,224},{224... | collective-permute-start | bytes 294920 | tf_op jit(solution)/shard_map/ppermute | solution.py:32
  186.7 11.4 %collective-permute-start.15 = (bf16[192,256]{1,0:T(8,128)(2,1)S(1)}, bf16[192,256]{1,0:T(8,128)(2,1)S(1)}, u32[]{:S(2)}, u32[]{:S(2)}) collective-permute-start(bf16[192,256]{1,0:T(8,128)(2,1)S(1)} %get-tuple-element.23), channel_id=1, source_target_pairs={{0,224},{32,0},{64,32},{96,64},{128,96},{160,128},{192,160},{224,1... | collective-permute-start | bytes 294920 | tf_op jit(solution)/shard_map/ppermute | solution.py:32
  198.1 3.1 %collective-permute-done.11 = bf16[192,256]{1,0:T(8,128)(2,1)S(1)} collective-permute-done((bf16[192,256]{1,0:T(8,128)(2,1)S(1)}, bf16[192,256]{1,0:T(8,128)(2,1)S(1)}, u32[]{:S(2)}, u32[]{:S(2)}) %collective-permute-start.11) | collective-permute-done | bytes 98336 | tf_op jit(solution)/shard_map/ppermute | solution.py:32
  201.5 3.3 %collective-permute-start.16 = (bf16[384,256]{1,0:T(8,128)(2,1)S(1)}, bf16[384,256]{1,0:T(8,128)(2,1)S(1)}, u32[]{:S(2)}, u32[]{:S(2)}) collective-permute-start(bf16[384,256]{1,0:T(8,128)(2,1)S(1)} %pad_maximum_fusion.1), channel_id=1, source_target_pairs={{0,224},{32,0},{64,32},{96,64},{128,96},{160,128},{192,160},{224,1... | collective-permute-start | bytes 589832 | tf_op jit(solution)/shard_map/ppermute | solution.py:32
  204.8 4.5 %collective-permute-done.12 = bf16[384,256]{1,0:T(8,128)(2,1)S(1)} collective-permute-done((bf16[384,256]{1,0:T(8,128)(2,1)S(1)}, bf16[384,256]{1,0:T(8,128)(2,1)S(1)}, u32[]{:S(2)}, u32[]{:S(2)}) %collective-permute-start.12) | collective-permute-done | bytes 196640 | tf_op jit(solution)/shard_map/ppermute | solution.py:32
  209.3 0.1 collective-permute-start.13
  209.4 6.9 %collective-permute-done.13 = bf16[384,256]{1,0:T(8,128)(2,1)S(1)} collective-permute-done((bf16[384,256]{1,0:T(8,128)(2,1)S(1)}, bf16[384,256]{1,0:T(8,128)(2,1)S(1)}, u32[]{:S(2)}, u32[]{:S(2)}) %collective-permute-start.13) | collective-permute-done | bytes 196640 | tf_op jit(solution)/shard_map/ppermute | solution.py:32
  216.2 0.1 add_convert_fusion.3
  216.3 0.4 collective-permute-start.17
  216.7 1.8 collective-permute-start.14
  218.5 3.6 %collective-permute-done.17 = bf16[384,256]{1,0:T(8,128)(2,1)S(1)} collective-permute-done((bf16[384,256]{1,0:T(8,128)(2,1)S(1)}, bf16[384,256]{1,0:T(8,128)(2,1)S(1)}, u32[]{:S(2)}, u32[]{:S(2)}) %collective-permute-start.17) | collective-permute-done | bytes 196640 | tf_op jit(solution)/shard_map/ppermute | solution.py:32
  222.2 1.6 collective-permute-start.18
  223.7 4.2 %collective-permute-done.18 = bf16[384,256]{1,0:T(8,128)(2,1)S(1)} collective-permute-done((bf16[384,256]{1,0:T(8,128)(2,1)S(1)}, bf16[384,256]{1,0:T(8,128)(2,1)S(1)}, u32[]{:S(2)}, u32[]{:S(2)}) %collective-permute-start.18) | collective-permute-done | bytes 196640 | tf_op jit(solution)/shard_map/ppermute | solution.py:32
  228.0 0.1 collective-permute-start.19
  228.1 8.4 %collective-permute-done.19 = bf16[192,256]{1,0:T(8,128)(2,1)S(1)} collective-permute-done((bf16[192,256]{1,0:T(8,128)(2,1)S(1)}, bf16[192,256]{1,0:T(8,128)(2,1)S(1)}, u32[]{:S(2)}, u32[]{:S(2)}) %collective-permute-start.19) | collective-permute-done | bytes 98336 | tf_op jit(solution)/shard_map/ppermute | solution.py:32
  236.5 0.6 fusion.20
  237.2 17.5 %reduce-scatter.4.cloned.1.call-done = bf16[640,192]{1,0:T(8,128)(2,1)} async-done(((bf16[5120,192]{1,0:T(8,128)(2,1)}), bf16[640,192]{1,0:T(8,128)(2,1)}) %reduce-scatter.4.cloned.1.call-update) | async-done | bytes 245776
  254.7 1.8 copy.11
  (54 shorter events, 1.0 us)
Async XLA Ops:
  7.2 56.0 %all-gather.5.cloned.1.call-start = ((), (), s32[]{:S(2)}) async-start(), calls=%async_computation.2 | async-start | bytes 2211840 | tf_op jit(solution)/shard_map/all_gather | solution.py:278
  7.9 154.2 %all-gather.3.cloned.1.call-start = ((), (), s32[]{:S(2)}) async-start(), calls=%async_computation.1 | async-start | bytes 6758400 | tf_op jit(solution)/shard_map/all_gather | solution.py:277
  8.6 246.0 %reduce-scatter.4.cloned.1.call-start = ((), (), s32[]{:S(2)}) async-start(), calls=%async_computation.3 | async-start | bytes 2949120
  10.3 6.2 %collective-permute-start = (bf16[192,256]{1,0:T(8,128)(2,1)S(1)}, bf16[192,256]{1,0:T(8,128)(2,1)S(1)}, u32[]{:S(2)}, u32[]{:S(2)}) collective-permute-start(bf16[192,256]{1,0:T(8,128)(2,1)S(1)} %constant_dynamic-update-slice_fusion), channel_id=1, source_target_pairs={{0,16},{16,0},{1,17},{17,1},{2,18},{18,2},{3,19},{19,3},{4,20},{20... | collective-permute-start | bytes 294920 | tf_op jit(solution)/shard_map/ppermute | solution.py:32
  16.6 9.7 %collective-permute-start.4 = (bf16[384,256]{1,0:T(8,128)(2,1)S(1)}, bf16[384,256]{1,0:T(8,128)(2,1)S(1)}, u32[]{:S(2)}, u32[]{:S(2)}) collective-permute-start(bf16[384,256]{1,0:T(8,128)(2,1)S(1)} %get-tuple-element.17), channel_id=1, source_target_pairs={{0,32},{32,64},{64,96},{96,128},{128,160},{160,192},{192,224},{224... | collective-permute-start | bytes 589832 | tf_op jit(solution)/shard_map/ppermute | solution.py:32
  18.6 7.7 %collective-permute-start.1 = (bf16[384,256]{1,0:T(8,128)(2,1)S(1)}, bf16[384,256]{1,0:T(8,128)(2,1)S(1)}, u32[]{:S(2)}, u32[]{:S(2)}) collective-permute-start(bf16[384,256]{1,0:T(8,128)(2,1)S(1)} %get-tuple-element.17), channel_id=1, source_target_pairs={{0,224},{32,0},{64,32},{96,64},{128,96},{160,128},{192,160},{224,1... | collective-permute-start | bytes 589832 | tf_op jit(solution)/shard_map/ppermute | solution.py:32
  26.3 6.9 %collective-permute-start.5 = (bf16[384,256]{1,0:T(8,128)(2,1)S(1)}, bf16[384,256]{1,0:T(8,128)(2,1)S(1)}, u32[]{:S(2)}, u32[]{:S(2)}) collective-permute-start(bf16[384,256]{1,0:T(8,128)(2,1)S(1)} %collective-permute-done.4), channel_id=1, source_target_pairs={{0,32},{32,64},{64,96},{96,128},{128,160},{160,192},{192,224},{224... | collective-permute-start | bytes 589832 | tf_op jit(solution)/shard_map/ppermute | solution.py:32
  26.3 6.9 %collective-permute-start.2 = (bf16[384,256]{1,0:T(8,128)(2,1)S(1)}, bf16[384,256]{1,0:T(8,128)(2,1)S(1)}, u32[]{:S(2)}, u32[]{:S(2)}) collective-permute-start(bf16[384,256]{1,0:T(8,128)(2,1)S(1)} %collective-permute-done.1), channel_id=1, source_target_pairs={{0,224},{32,0},{64,32},{96,64},{128,96},{160,128},{192,160},{224,1... | collective-permute-start | bytes 589832 | tf_op jit(solution)/shard_map/ppermute | solution.py:32
  33.2 6.9 %collective-permute-start.6 = (bf16[384,256]{1,0:T(8,128)(2,1)S(1)}, bf16[384,256]{1,0:T(8,128)(2,1)S(1)}, u32[]{:S(2)}, u32[]{:S(2)}) collective-permute-start(bf16[384,256]{1,0:T(8,128)(2,1)S(1)} %collective-permute-done.5), channel_id=1, source_target_pairs={{0,32},{32,64},{64,96},{96,128},{128,160},{160,192},{192,224},{224... | collective-permute-start | bytes 589832 | tf_op jit(solution)/shard_map/ppermute | solution.py:32
  33.2 7.0 %collective-permute-start.3 = (bf16[384,256]{1,0:T(8,128)(2,1)S(1)}, bf16[384,256]{1,0:T(8,128)(2,1)S(1)}, u32[]{:S(2)}, u32[]{:S(2)}) collective-permute-start(bf16[384,256]{1,0:T(8,128)(2,1)S(1)} %collective-permute-done.2), channel_id=1, source_target_pairs={{0,224},{32,0},{64,32},{96,64},{128,96},{160,128},{192,160},{224,1... | collective-permute-start | bytes 589832 | tf_op jit(solution)/shard_map/ppermute | solution.py:32
  36.4 10.1 %copy-start.3 = (s32[4]{0:T(128)S(1)}, s32[4]{0:T(128)}, u32[]{:S(2)}) copy-start(s32[4]{0:T(128)} %param.11) | copy-start | bytes 52
  36.4 14.3 %copy-start.2 = (bf16[192,640]{1,0:T(8,128)(2,1)S(1)}, bf16[192,640]{1,0:T(8,128)(2,1)}, u32[]{:S(2)}) copy-start(bf16[192,640]{1,0:T(8,128)(2,1)} %q_ref.3) | copy-start | bytes 737284
  40.0 5.9 %collective-permute-start.7 = (bf16[192,256]{1,0:T(8,128)(2,1)S(1)}, bf16[192,256]{1,0:T(8,128)(2,1)S(1)}, u32[]{:S(2)}, u32[]{:S(2)}) collective-permute-start(bf16[192,256]{1,0:T(8,128)(2,1)S(1)} %slice.89), channel_id=1, source_target_pairs={{0,32},{32,64},{64,96},{96,128},{128,160},{160,192},{192,224},{224... | collective-permute-start | bytes 294920 | tf_op jit(solution)/shard_map/ppermute | solution.py:32
  40.2 5.8 %collective-permute-start.8 = (bf16[192,256]{1,0:T(8,128)(2,1)S(1)}, bf16[192,256]{1,0:T(8,128)(2,1)S(1)}, u32[]{:S(2)}, u32[]{:S(2)}) collective-permute-start(bf16[192,256]{1,0:T(8,128)(2,1)S(1)} %slice.90), channel_id=1, source_target_pairs={{0,224},{32,0},{64,32},{96,64},{128,96},{160,128},{192,160},{224,1... | collective-permute-start | bytes 294920 | tf_op jit(solution)/shard_map/ppermute | solution.py:32
  46.1 8.8 %copy-start = (bf16[3072,256]{1,0:T(8,128)(2,1)}, bf16[3072,256]{1,0:T(8,128)(2,1)S(1)}, u32[]{:S(2)}) copy-start(bf16[3072,256]{1,0:T(8,128)(2,1)S(1)} %constant_dynamic-update-slice_fusion.2.mine_ref) | copy-start | bytes 4718596
  46.1 4.4 %collective-permute-start.9 = (bf16[3072,256]{1,0:T(8,128)(2,1)S(1)}, bf16[3072,256]{1,0:T(8,128)(2,1)}, u32[]{:S(2)}, u32[]{:S(2)}) collective-permute-start(bf16[3072,256]{1,0:T(8,128)(2,1)S(1)} %constant_dynamic-update-slice_fusion.2.mine_ref), channel_id=1, source_target_pairs={{0,8},{8,0},{1,9},{9,1},{2,10},{10,2},{3,11},{11,3},{4,12},{12,4},... | collective-permute-start | bytes 4718600 | tf_op jit(solution)/shard_map/ppermute | solution.py:32
  162.1 5.3 %copy-start.1 = (bf16[3072,256]{1,0:T(8,128)(2,1)S(1)}, bf16[3072,256]{1,0:T(8,128)(2,1)}, u32[]{:S(2)}) copy-start(bf16[3072,256]{1,0:T(8,128)(2,1)} %copy-done) | copy-start | bytes 4718596
  162.1 11.3 %slice-start = ((s8[6553600]{0:T(1024)(128)(4,1)}), s8[4194304]{0:T(1024)(128)(4,1)S(1)}, s32[]{:S(2)}) async-start(s8[6553600]{0:T(1024)(128)(4,1)} %bitcast.13), calls=%async_computation.4 | async-start | bytes 8388608
  167.5 6.0 %slice-start.1 = ((s8[6553600]{0:T(1024)(128)(4,1)}), s8[2359296]{0:T(1024)(128)(4,1)S(1)}, s32[]{:S(2)}) async-start(s8[6553600]{0:T(1024)(128)(4,1)} %bitcast.13), calls=%async_computation.5 | async-start | bytes 4718592
  173.2 8.2 %collective-permute-start.10 = (bf16[3072,256]{1,0:T(8,128)(2,1)}, bf16[3072,256]{1,0:T(8,128)(2,1)}, u32[]{:S(2)}, u32[]{:S(2)}) collective-permute-start(bf16[3072,256]{1,0:T(8,128)(2,1)} %get-tuple-element.15), channel_id=1, source_target_pairs={{0,8},{8,0},{1,9},{9,1},{2,10},{10,2},{3,11},{11,3},{4,12},{12,4},... | collective-permute-start | bytes 4718600 | tf_op jit(solution)/shard_map/ppermute | solution.py:32
  183.3 17.9 %collective-permute-start.11 = (bf16[192,256]{1,0:T(8,128)(2,1)S(1)}, bf16[192,256]{1,0:T(8,128)(2,1)S(1)}, u32[]{:S(2)}, u32[]{:S(2)}) collective-permute-start(bf16[192,256]{1,0:T(8,128)(2,1)S(1)} %get-tuple-element.22), channel_id=1, source_target_pairs={{0,32},{32,64},{64,96},{96,128},{128,160},{160,192},{192,224},{224... | collective-permute-start | bytes 294920 | tf_op jit(solution)/shard_map/ppermute | solution.py:32
  186.7 14.6 %collective-permute-start.15 = (bf16[192,256]{1,0:T(8,128)(2,1)S(1)}, bf16[192,256]{1,0:T(8,128)(2,1)S(1)}, u32[]{:S(2)}, u32[]{:S(2)}) collective-permute-start(bf16[192,256]{1,0:T(8,128)(2,1)S(1)} %get-tuple-element.23), channel_id=1, source_target_pairs={{0,224},{32,0},{64,32},{96,64},{128,96},{160,128},{192,160},{224,1... | collective-permute-start | bytes 294920 | tf_op jit(solution)/shard_map/ppermute | solution.py:32
  201.3 7.9 %collective-permute-start.12 = (bf16[384,256]{1,0:T(8,128)(2,1)S(1)}, bf16[384,256]{1,0:T(8,128)(2,1)S(1)}, u32[]{:S(2)}, u32[]{:S(2)}) collective-permute-start(bf16[384,256]{1,0:T(8,128)(2,1)S(1)} %pad_maximum_fusion), channel_id=1, source_target_pairs={{0,32},{32,64},{64,96},{96,128},{128,160},{160,192},{192,224},{224... | collective-permute-start | bytes 589832 | tf_op jit(solution)/shard_map/ppermute | solution.py:32
  201.5 7.9 %collective-permute-start.16 = (bf16[384,256]{1,0:T(8,128)(2,1)S(1)}, bf16[384,256]{1,0:T(8,128)(2,1)S(1)}, u32[]{:S(2)}, u32[]{:S(2)}) collective-permute-start(bf16[384,256]{1,0:T(8,128)(2,1)S(1)} %pad_maximum_fusion.1), channel_id=1, source_target_pairs={{0,224},{32,0},{64,32},{96,64},{128,96},{160,128},{192,160},{224,1... | collective-permute-start | bytes 589832 | tf_op jit(solution)/shard_map/ppermute | solution.py:32
  209.3 7.0 %collective-permute-start.13 = (bf16[384,256]{1,0:T(8,128)(2,1)S(1)}, bf16[384,256]{1,0:T(8,128)(2,1)S(1)}, u32[]{:S(2)}, u32[]{:S(2)}) collective-permute-start(bf16[384,256]{1,0:T(8,128)(2,1)S(1)} %add_convert_fusion.4), channel_id=1, source_target_pairs={{0,32},{32,64},{64,96},{96,128},{128,160},{160,192},{192,224},{224... | collective-permute-start | bytes 589832 | tf_op jit(solution)/shard_map/ppermute | solution.py:32
  216.3 5.7 %collective-permute-start.17 = (bf16[384,256]{1,0:T(8,128)(2,1)S(1)}, bf16[384,256]{1,0:T(8,128)(2,1)S(1)}, u32[]{:S(2)}, u32[]{:S(2)}) collective-permute-start(bf16[384,256]{1,0:T(8,128)(2,1)S(1)} %get-tuple-element.19), channel_id=1, source_target_pairs={{0,224},{32,0},{64,32},{96,64},{128,96},{160,128},{192,160},{224,1... | collective-permute-start | bytes 589832 | tf_op jit(solution)/shard_map/ppermute | solution.py:32
  216.7 7.0 %collective-permute-start.14 = (bf16[384,256]{1,0:T(8,128)(2,1)S(1)}, bf16[384,256]{1,0:T(8,128)(2,1)S(1)}, u32[]{:S(2)}, u32[]{:S(2)}) collective-permute-start(bf16[384,256]{1,0:T(8,128)(2,1)S(1)} %get-tuple-element.18), channel_id=1, source_target_pairs={{0,32},{32,64},{64,96},{96,128},{128,160},{160,192},{192,224},{224... | collective-permute-start | bytes 589832 | tf_op jit(solution)/shard_map/ppermute | solution.py:32
  222.2 5.7 %collective-permute-start.18 = (bf16[384,256]{1,0:T(8,128)(2,1)S(1)}, bf16[384,256]{1,0:T(8,128)(2,1)S(1)}, u32[]{:S(2)}, u32[]{:S(2)}) collective-permute-start(bf16[384,256]{1,0:T(8,128)(2,1)S(1)} %add_convert_fusion.1), channel_id=1, source_target_pairs={{0,224},{32,0},{64,32},{96,64},{128,96},{160,128},{192,160},{224,1... | collective-permute-start | bytes 589832 | tf_op jit(solution)/shard_map/ppermute | solution.py:32
  228.0 8.5 %collective-permute-start.19 = (bf16[192,256]{1,0:T(8,128)(2,1)S(1)}, bf16[192,256]{1,0:T(8,128)(2,1)S(1)}, u32[]{:S(2)}, u32[]{:S(2)}) collective-permute-start(bf16[192,256]{1,0:T(8,128)(2,1)S(1)} %select_convert_fusion), channel_id=1, source_target_pairs={{0,16},{16,0},{1,17},{17,1},{2,18},{18,2},{3,19},{19,3},{4,20},{20... | collective-permute-start | bytes 294920 | tf_op jit(solution)/shard_map/ppermute | solution.py:32
Sparse Core Ops, SparseCore 0:
  9.8 53.3 all-gather.4
  66.0 96.1 all-gather.2
  181.6 73.0 reduce-scatter.3
